TPU v7x, 128 devices: a whole 4x4x4 slice. The times are simulated.
128 devices in a mesh: dp: 16 (over x, y), expert: 8 (over z, core).
Axes of the slice: x: 4, y: 4, z: 4, core: 2. Of those that a mesh axis runs over, the one named last changes fastest.
Arguments:
- layer_input: bfloat16 [16384, 2560], P(('dp', 'expert')), may hold values from -6 to 6
- output_grad: bfloat16 [16384, 2560], P(('dp', 'expert')), may hold values from -6 to 6
- expert_ids: int32 [16384, 2], P(('dp', 'expert')), may hold values from 0 to 7, all different within a row; in each aligned block of 128 rows (0 to 127, 128 to 255, ...) at most 48 rows name the same one
- gate_probs: bfloat16 [16384, 2], P(('dp', 'expert')), may hold values from 0.099609375 to 0.59765625
- gate_weight: float32 [8, 2560, 1536], P('expert', 'dp'), may hold values from -0.125 to 0.125
- up_weight: float32 [8, 2560, 1536], P('expert', 'dp'), may hold values from -0.125 to 0.125
- down_weight: float32 [8, 1536, 2560], P('expert', 'dp'), may hold values from -0.15625 to 0.15625
- gate_moment: float32 [8, 2560, 1536], P('expert', 'dp'), may hold values from -12 to 12
- up_moment: float32 [8, 2560, 1536], P('expert', 'dp'), may hold values from -12 to 12
- down_moment: float32 [8, 1536, 2560], P('expert', 'dp'), may hold values from -12 to 12
- gate_second: float32 [8, 2560, 1536], P('expert', 'dp'), may hold values from 1 to 100
- up_second: float32 [8, 2560, 1536], P('expert', 'dp'), may hold values from 1 to 100
- down_second: float32 [8, 1536, 2560], P('expert', 'dp'), may hold values from 1 to 100
Outputs:
- input_grad: bfloat16 [16384, 2560], P(('dp', 'expert'))
- prob_grad: bfloat16 [16384, 2], P(('dp', 'expert'))
- new_gate_weight: float32 [8, 2560, 1536], P('expert', 'dp')
- new_up_weight: float32 [8, 2560, 1536], P('expert', 'dp')
- new_down_weight: float32 [8, 1536, 2560], P('expert', 'dp')
- new_gate_moment: float32 [8, 2560, 1536], P('expert', 'dp')
- new_up_moment: float32 [8, 2560, 1536], P('expert', 'dp')
- new_down_moment: float32 [8, 1536, 2560], P('expert', 'dp')
- new_gate_second: float32 [8, 2560, 1536], P('expert', 'dp')
- new_up_second: float32 [8, 2560, 1536], P('expert', 'dp')
- new_down_second: float32 [8, 1536, 2560], P('expert', 'dp')
Inputs may be any that keep to these rules, and one draw needn't show every extreme that they name: `expert_ids`: each token names 2 different experts. Among the (token, pick) pairs of one device's 128 tokens, no expert is named more than 48 times, and in every draw some device's tokens name some expert exactly 48 times.
All inputs are finite; a program needn't handle non-finite values.
Results may differ from a plain program's by a relative error of at most 0.025.
Values may be sent and summed in bfloat16 or wider, within the bound.
No kernel may reach another device: no remote copies, remote signals or barrier semaphores. Data moves between devices by JAX's collectives and lax.ppermute only.
A program may use at most 256 MiB of HBM per device.

v0:
```python
import jax
import jax.numpy as jnp
from jax import lax
from jax.sharding import PartitionSpec as P

beta_one = 0.9
beta_two = 0.95
learn_rate = 0.003
decay_rate = 0.1
epsilon = 1e-08
correct_one = 1.0 - 2.6561398887587e-05
correct_two = 1.0 - 0.005920529220333


def slot_tables(flat_ids, expert_count, exp_dev, groups, capacity):
    onehot = (flat_ids[:, None] == jnp.arange(expert_count, dtype=jnp.int32)[None, :]).astype(
        jnp.int32
    )
    before = jnp.cumsum(onehot, axis=0) - onehot
    ranked = jnp.sum(before * onehot, axis=1)
    device = flat_ids // exp_dev
    local = flat_ids % exp_dev
    return (local * groups + device) * capacity + ranked


def adamw(weight, moment, second, grad):
    moment_new = beta_one * moment + (1.0 - beta_one) * grad
    second_new = beta_two * second + (1.0 - beta_two) * grad * grad
    update = moment_new / correct_one / (jnp.sqrt(second_new / correct_two) + epsilon)
    return (weight - learn_rate * (update + decay_rate * weight), moment_new, second_new)


def body(
    layer_input,
    output_grad,
    expert_ids,
    gate_probs,
    gate_weight,
    up_weight,
    down_weight,
    gate_moment,
    up_moment,
    down_moment,
    gate_second,
    up_second,
    down_second,
):
    exp_dev = gate_weight.shape[0]
    hidden_units = gate_weight.shape[2]
    width = layer_input.shape[1]
    groups = lax.axis_size("expert")
    tok_count, picks = expert_ids.shape
    capacity = 3 * tok_count * picks // (2 * exp_dev * groups)
    slots = exp_dev * groups * capacity
    row_count = groups * capacity
    dest_slot = slot_tables(expert_ids.reshape(-1), exp_dev * groups, exp_dev, groups, capacity)
    owner = (
        jnp.zeros((slots,), jnp.int32)
        .at[dest_slot]
        .set(jnp.arange(tok_count * picks, dtype=jnp.int32) // picks)
    )
    filled = jnp.zeros((slots,), jnp.int32).at[dest_slot].set(1) > 0
    zero_val = jnp.zeros((), jnp.bfloat16)
    send_input = jnp.where(filled[:, None], layer_input[owner], zero_val).reshape(
        exp_dev, groups, capacity, width
    )
    send_grad = jnp.where(filled[:, None], output_grad[owner], zero_val).reshape(
        exp_dev, groups, capacity, width
    )
    send_gate = (
        jnp.zeros((slots,), jnp.bfloat16)
        .at[dest_slot]
        .set(gate_probs.reshape(-1))
        .reshape(exp_dev, groups, capacity)
    )
    w_gate_up_shard = jnp.concatenate((gate_weight, up_weight), axis=2).astype(jnp.bfloat16)
    w_down_shard = down_weight.astype(jnp.bfloat16)
    w_gate_up, w_down = (
        lax.all_gather(w_gate_up_shard, "dp", axis=1, tiled=True),
        lax.all_gather(w_down_shard, "dp", axis=1, tiled=True),
    )
    recv_input, recv_grad, recv_gate = (
        lax.all_to_all(send_input, "expert", split_axis=1, concat_axis=1, tiled=True),
        lax.all_to_all(send_grad, "expert", split_axis=1, concat_axis=1, tiled=True),
        lax.all_to_all(send_gate, "expert", split_axis=1, concat_axis=1, tiled=True),
    )
    x_rows = recv_input.reshape(exp_dev, row_count, width)
    dy_rows = recv_grad.reshape(exp_dev, row_count, width)
    gate_rows = recv_gate.reshape(exp_dev, row_count)
    pre = jnp.einsum("erd,edf->erf", x_rows, w_gate_up, preferred_element_type=jnp.float32)
    gate_pre = pre[:, :, :hidden_units]
    up_pre = pre[:, :, hidden_units:]
    sigmoid_gate = jax.nn.sigmoid(gate_pre)
    silu_gate = gate_pre * sigmoid_gate
    hidden_full = silu_gate * up_pre
    hidden = hidden_full.astype(jnp.bfloat16)
    gate_col = gate_rows.astype(jnp.float32)[:, :, None]
    raw_grad = jnp.einsum("erd,efd->erf", dy_rows, w_down, preferred_element_type=jnp.float32)
    prob_rows = jnp.sum(hidden.astype(jnp.float32) * raw_grad, axis=2).astype(jnp.bfloat16)
    hidden_scaled = (gate_col * hidden_full).astype(jnp.bfloat16)
    hidden_grad = gate_col * raw_grad
    dsilu = sigmoid_gate * (1.0 + gate_pre * (1.0 - sigmoid_gate))
    pre_grad = jnp.concatenate(
        (hidden_grad * up_pre * dsilu, hidden_grad * silu_gate), axis=2
    ).astype(jnp.bfloat16)
    input_rows = jnp.einsum(
        "erf,edf->erd", pre_grad, w_gate_up, preferred_element_type=jnp.float32
    ).astype(jnp.bfloat16)
    second = jnp.einsum(
        "erc,erd->ecd", hidden_scaled, dy_rows, preferred_element_type=jnp.float32
    ).astype(jnp.bfloat16)
    first = jnp.einsum("erc,erf->ecf", x_rows, pre_grad, preferred_element_type=jnp.float32).astype(
        jnp.bfloat16
    )
    grad_down = lax.psum_scatter(second[0], "dp", scatter_dimension=0, tiled=True)[None].astype(
        jnp.float32
    )
    grad_gate_up = lax.psum_scatter(first[0], "dp", scatter_dimension=0, tiled=True)[None].astype(
        jnp.float32
    )
    back_input, back_prob = (
        lax.all_to_all(
            input_rows.reshape(exp_dev, groups, capacity, width),
            "expert",
            split_axis=1,
            concat_axis=1,
            tiled=True,
        ),
        lax.all_to_all(
            prob_rows.reshape(exp_dev, groups, capacity),
            "expert",
            split_axis=1,
            concat_axis=1,
            tiled=True,
        ),
    )
    picked_rows = back_input.reshape(slots, width)[dest_slot].reshape(tok_count, picks, width)
    input_grad = jnp.sum(picked_rows.astype(jnp.float32), axis=1).astype(jnp.bfloat16)
    prob_grad = back_prob.reshape(slots)[dest_slot].reshape(tok_count, picks)
    new_gate_weight, new_gate_moment, new_gate_second = adamw(
        gate_weight, gate_moment, gate_second, grad_gate_up[:, :, :hidden_units]
    )
    new_up_weight, new_up_moment, new_up_second = adamw(
        up_weight, up_moment, up_second, grad_gate_up[:, :, hidden_units:]
    )
    new_down_weight, new_down_moment, new_down_second = adamw(
        down_weight, down_moment, down_second, grad_down
    )
    return (
        input_grad,
        prob_grad,
        new_gate_weight,
        new_up_weight,
        new_down_weight,
        new_gate_moment,
        new_up_moment,
        new_down_moment,
        new_gate_second,
        new_up_second,
        new_down_second,
    )


def solution(mesh):
    return jax.shard_map(
        body,
        mesh=mesh,
        in_specs=(
            P(("dp", "expert"), None),
            P(("dp", "expert"), None),
            P(("dp", "expert"), None),
            P(("dp", "expert"), None),
            P("expert", "dp", None),
            P("expert", "dp", None),
            P("expert", "dp", None),
            P("expert", "dp", None),
            P("expert", "dp", None),
            P("expert", "dp", None),
            P("expert", "dp", None),
            P("expert", "dp", None),
            P("expert", "dp", None),
        ),
        out_specs=(
            P(("dp", "expert"), None),
            P(("dp", "expert"), None),
            P("expert", "dp", None),
            P("expert", "dp", None),
            P("expert", "dp", None),
            P("expert", "dp", None),
            P("expert", "dp", None),
            P("expert", "dp", None),
            P("expert", "dp", None),
            P("expert", "dp", None),
            P("expert", "dp", None),
        ),
        check_vma=False,
    )
```

profile of v0, /device:TPU:1, one launch (start us, length us, event | category | flops | bytes accessed | tf_op | source)
XLA Modules:
  0.0 440.1 jit_solution(14314940471210939129)
XLA Ops:
  12.8 2.2 scatter_custom_fusion
  15.7 6.8 %all-to-all-start = ((bf16[1,8,48]{2,0,1:T(2,128)(2,1)}), bf16[1,8,48]{2,0,1:T(2,128)(2,1)S(1)}, u32[]{:S(2)}, u32[]{:S(2)}) async-start(bf16[1,8,48]{2,0,1:T(2,128)(2,1)} %reshape.315), calls=%async_computation | async-start | bytes 8192 | tf_op jit(solution)/shard_map/all_to_all | solution.py:85
  25.5 3.3 gather_fusion.1
  28.8 3.3 gather_fusion
  32.0 3.8 broadcast_select_fusion
  35.9 29.9 %all_to_all.25 = bf16[1,8,48,2560]{3,2,0,1:T(8,128)(2,1)} all-to-all(bf16[1,8,48,2560]{3,2,0,1:T(8,128)(2,1)S(1)} %get-tuple-element.60), channel_id=1, replica_groups=mesh['dp'=16,'expert'=8] {'expert'}, dimensions={1} | all-to-all | bytes 3932160 | tf_op jit(solution)/shard_map/all_to_all | solution.py:83
  65.8 5.2 %all-to-all-start.1 = ((bf16[1,8,48,2560]{3,2,0,1:T(8,128)(2,1)}), bf16[1,8,48,2560]{3,2,0,1:T(8,128)(2,1)}, u32[]{:S(2)}, u32[]{:S(2)}) async-start(bf16[1,8,48,2560]{3,2,0,1:T(8,128)(2,1)} %get-tuple-element.61), calls=%async_computation.1 | async-start | bytes 3932160 | tf_op jit(solution)/shard_map/all_to_all | solution.py:84
  71.1 49.0 %all-gather.5.cloned.1.call-done = bf16[1,2560,3072]{2,1,0:T(8,128)(2,1)} async-done(((bf16[1,160,3072]{2,1,0:T(8,128)(2,1)}), bf16[1,2560,3072]{2,1,0:T(8,128)(2,1)}) %all-gather.5.cloned.1.call-update) | async-done | bytes 15728656 | tf_op jit(solution)/shard_map/all_gather | solution.py:79
  120.1 12.2 %fusion.6 = f32[1,384,3072]{2,1,0:T(8,128)} fusion(bf16[384,2560]{1,0:T(8,128)(2,1)S(1)} %bitcast.82, bf16[1,2560,3072]{2,1,0:T(8,128)(2,1)} %all-gather.5.cloned.1.call-done), kind=kOutput, calls=%fused_computation.15 | convolution fusion | flops 6039797760 | bytes 22413312 | tf_op jit(solution)/shard_map/erd,edf->erf/dot_general | solution.py:90
  132.3 10.6 %convolution_convert_fusion.1 = bf16[1536,2560]{1,0:T(8,128)(2,1)} fusion(bf16[384,2560]{1,0:T(8,128)(2,1)} %bitcast.6, f32[384]{0:T(512)S(1)} %reshape.255, f32[1,384,3072]{2,1,0:T(8,128)} %fusion.6), kind=kOutput, calls=%fused_computation.12 | convolution fusion | flops 3027959808 | bytes 14550528 | tf_op jit(solution)/shard_map/erc,erd->ecd/dot_general | solution.py:109
  142.9 82.5 %reduce-scatter.5.cloned.1.call-done = bf16[96,2560]{1,0:T(8,128)(2,1)} async-done(((bf16[1536,2560]{1,0:T(8,128)(2,1)}), bf16[96,2560]{1,0:T(8,128)(2,1)}) %reduce-scatter.5.cloned.1.call-update) | async-done | bytes 491536 | tf_op jit(solution)/shard_map/reduce_scatter | solution.py:115
  225.4 4.5 %multiply_subtract_fusion = (f32[1,96,2560]{2,1,0:T(8,128)}, f32[1,96,2560]{2,1,0:T(8,128)}, f32[1,96,2560]{2,1,0:T(8,128)}, bf16[1,96,2560]{2,1,0:T(8,128)(2,1)}) fusion(f32[1,96,2560]{2,1,0:T(8,128)} %param.19, bf16[96,2560]{1,0:T(8,128)(2,1)} %reduce-scatter.5.cloned.1.call-done, f32[1,96,2560]{2,1,0:T(8,128)} %param.22, f32[1,96,2560]{2,1,0:T(8,128)} %param.25), kind=kLoop, calls=%fused_computation.47 | loop fusion | flops 4177920 | bytes 6881280 | tf_op jit(solution)/shard_map/sub | solution.py:30
  230.2 68.9 %all-gather.3.cloned.1.call-done = bf16[1,1536,2560]{2,1,0:T(8,128)(2,1)} async-done(((bf16[1,96,2560]{2,1,0:T(8,128)(2,1)}), bf16[1,1536,2560]{2,1,0:T(8,128)(2,1)}) %all-gather.3.cloned.1.call-update) | async-done | bytes 7864336 | tf_op jit(solution)/shard_map/all_gather | solution.py:80
  299.1 9.1 %fusion.21 = (bf16[384,1536]{1,0:T(8,128)(2,1)S(1)}, bf16[384,1536]{1,0:T(8,128)(2,1)S(1)}, bf16[384]{0:T(512)(128)(2,1)S(1)}) fusion(f32[1,384,3072]{2,1,0:T(8,128)} %fusion.6, f32[384]{0:T(512)S(1)} %reshape.255, bf16[384,2560]{1,0:T(8,128)(2,1)} %bitcast.6, bf16[1,1536,2560]{2,1,0:T(8,128)(2,1)} %all-gather.3.cloned.1.call-done), kind=kOutput, calls=%fused_computation.38 | convolution fusion | flops 3031105024 | bytes 16910592 | tf_op jit(solution)/shard_map/erd,efd->erf/dot_general | solution.py:98
  309.7 11.5 %convolution_convert_fusion = bf16[2560,3072]{1,0:T(8,128)(2,1)} fusion(bf16[384,2560]{1,0:T(8,128)(2,1)S(1)} %bitcast.83, bf16[384,1536]{1,0:T(8,128)(2,1)S(1)} %get-tuple-element.54, bf16[384,1536]{1,0:T(8,128)(2,1)S(1)} %get-tuple-element.53), kind=kOutput, calls=%fused_computation.7 | convolution fusion | flops 6052380672 | bytes 20054016 | tf_op jit(solution)/shard_map/erc,erf->ecf/dot_general | solution.py:112
  321.9 5.1 %all-to-all-start.4 = ((bf16[1,8,48]{2,0,1:T(2,128)(2,1)}), bf16[1,8,48]{2,0,1:T(2,128)(2,1)S(1)}, u32[]{:S(2)}, u32[]{:S(2)}) async-start(bf16[1,8,48]{2,0,1:T(2,128)(2,1)} %convert_element_type.102), calls=%async_computation.4 | async-start | bytes 8192 | tf_op jit(solution)/shard_map/all_to_all | solution.py:129
  327.0 11.0 %fusion.9 = bf16[384,2560]{1,0:T(8,128)(2,1)} fusion(bf16[1,2560,3072]{2,1,0:T(8,128)(2,1)} %all-gather.5.cloned.1.call-done, bf16[384,1536]{1,0:T(8,128)(2,1)} %copy-done.10, bf16[384,1536]{1,0:T(8,128)(2,1)S(1)} %copy-done.9), kind=kOutput, calls=%fused_computation.16 | convolution fusion | flops 6045499392 | bytes 20054016 | tf_op jit(solution)/shard_map/erf,edf->erd/dot_general | solution.py:106
  338.0 4.8 %all-to-all-start.3 = ((bf16[1,8,48,2560]{3,2,0,1:T(8,128)(2,1)}), bf16[1,8,48,2560]{3,2,0,1:T(8,128)(2,1)S(1)}, u32[]{:S(2)}, u32[]{:S(2)}) async-start(bf16[1,8,48,2560]{3,2,0,1:T(8,128)(2,1)} %bitcast.84), calls=%async_computation.3 | async-start | bytes 3932160 | tf_op jit(solution)/shard_map/all_to_all | solution.py:122
  345.6 22.1 %all-to-all-done.3 = bf16[1,8,48,2560]{3,2,0,1:T(8,128)(2,1)S(1)} async-done(((bf16[1,8,48,2560]{3,2,0,1:T(8,128)(2,1)}), bf16[1,8,48,2560]{3,2,0,1:T(8,128)(2,1)S(1)}, u32[]{:S(2)}, u32[]{:S(2)}) %all-to-all-start.3) | async-done | bytes 1966112 | tf_op jit(solution)/shard_map/all_to_all | solution.py:122
  367.7 2.5 gather_fusion.2
  370.3 3.1 reshape.251
  373.4 4.4 reduce_sum.34
  377.7 48.6 %reduce-scatter.3.cloned.1.call-done = bf16[160,3072]{1,0:T(8,128)(2,1)} async-done(((bf16[2560,3072]{1,0:T(8,128)(2,1)}), bf16[160,3072]{1,0:T(8,128)(2,1)}) %reduce-scatter.3.cloned.1.call-update) | async-done | bytes 983056 | tf_op jit(solution)/shard_map/reduce_scatter | solution.py:118
  427.8 5.8 %multiply_subtract_fusion.1 = (f32[1,160,1536]{2,1,0:T(8,128)}, f32[1,160,1536]{2,1,0:T(8,128)}, f32[1,160,1536]{2,1,0:T(8,128)}, f32[1,160,1536]{2,1,0:T(8,128)...) fusion(f32[1,160,1536]{2,1,0:T(8,128)S(1)} %copy-done.3, f32[1,160,3072]{2,1,0:T(8,128)S(1)} %bitcast_convert_fusion, ...), kind=kLoop, calls=%fused_computation.48 | loop fusion | flops 7372800 | bytes 13762560 | tf_op jit(solution)/shard_map/sub | solution.py:30
  (70 shorter events, 16.0 us)
Async XLA Ops:
  7.2 18.3 %copy-start = (bf16[128,2560]{1,0:T(8,128)(2,1)S(1)}, bf16[128,2560]{1,0:T(8,128)(2,1)}, u32[]{:S(2)}) copy-start(bf16[128,2560]{1,0:T(8,128)(2,1)} %param.13) | copy-start | bytes 1966084
  7.2 112.9 %all-gather.5.cloned.1.call-start = ((), (), s32[]{:S(2)}) async-start(), calls=%async_computation.8 | async-start | bytes 16711680 | tf_op jit(solution)/shard_map/all_gather | solution.py:79
  8.6 2.4 copy-start.6
  8.6 3.9 copy-start.7
  15.7 20.2 %all-to-all-start = ((bf16[1,8,48]{2,0,1:T(2,128)(2,1)}), bf16[1,8,48]{2,0,1:T(2,128)(2,1)S(1)}, u32[]{:S(2)}, u32[]{:S(2)}) async-start(bf16[1,8,48]{2,0,1:T(2,128)(2,1)} %reshape.315), calls=%async_computation | async-start | bytes 8192 | tf_op jit(solution)/shard_map/all_to_all | solution.py:85
  25.5 3.3 copy-start.2
  65.8 54.3 %copy-start.5 = (bf16[1,8,48,2560]{3,2,0,1:T(8,128)(2,1)S(1)}, bf16[1,8,48,2560]{3,2,0,1:T(8,128)(2,1)}, u32[]{:S(2)}) copy-start(bf16[1,8,48,2560]{3,2,0,1:T(8,128)(2,1)} %all_to_all.25) | copy-start | bytes 5898244
  65.8 66.5 %all-to-all-start.1 = ((bf16[1,8,48,2560]{3,2,0,1:T(8,128)(2,1)}), bf16[1,8,48,2560]{3,2,0,1:T(8,128)(2,1)}, u32[]{:S(2)}, u32[]{:S(2)}) async-start(bf16[1,8,48,2560]{3,2,0,1:T(8,128)(2,1)} %get-tuple-element.61), calls=%async_computation.1 | async-start | bytes 3932160 | tf_op jit(solution)/shard_map/all_to_all | solution.py:84
  71.0 154.4 %reduce-scatter.5.cloned.1.call-start = ((), (), s32[]{:S(2)}) async-start(), calls=%async_computation.10 | async-start | bytes 8355840 | tf_op jit(solution)/shard_map/reduce_scatter | solution.py:115
  142.8 156.3 %all-gather.3.cloned.1.call-start = ((), (), s32[]{:S(2)}) async-start(), calls=%async_computation.7 | async-start | bytes 8355840 | tf_op jit(solution)/shard_map/all_gather | solution.py:80
  229.9 196.4 %reduce-scatter.3.cloned.1.call-start = ((), (), s32[]{:S(2)}) async-start(), calls=%async_computation.9 | async-start | bytes 16711680 | tf_op jit(solution)/shard_map/reduce_scatter | solution.py:118
  308.3 1.0 copy-start.8
  308.3 1.4 copy-start.10
  321.2 5.8 %copy-start.9 = (bf16[384,1536]{1,0:T(8,128)(2,1)S(1)}, bf16[384,1536]{1,0:T(8,128)(2,1)}, u32[]{:S(2)}) copy-start(bf16[384,1536]{1,0:T(8,128)(2,1)} %copy-done.8) | copy-start | bytes 3538948
  321.9 16.1 %all-to-all-start.4 = ((bf16[1,8,48]{2,0,1:T(2,128)(2,1)}), bf16[1,8,48]{2,0,1:T(2,128)(2,1)S(1)}, u32[]{:S(2)}, u32[]{:S(2)}) async-start(bf16[1,8,48]{2,0,1:T(2,128)(2,1)} %convert_element_type.102), calls=%async_computation.4 | async-start | bytes 8192 | tf_op jit(solution)/shard_map/all_to_all | solution.py:129
  338.0 29.7 %all-to-all-start.3 = ((bf16[1,8,48,2560]{3,2,0,1:T(8,128)(2,1)}), bf16[1,8,48,2560]{3,2,0,1:T(8,128)(2,1)S(1)}, u32[]{:S(2)}, u32[]{:S(2)}) async-start(bf16[1,8,48,2560]{3,2,0,1:T(8,128)(2,1)} %bitcast.84), calls=%async_computation.3 | async-start | bytes 3932160 | tf_op jit(solution)/shard_map/all_to_all | solution.py:122
  373.4 54.4 %copy-start.3 = (f32[1,160,1536]{2,1,0:T(8,128)S(1)}, f32[1,160,1536]{2,1,0:T(8,128)}, u32[]{:S(2)}) copy-start(f32[1,160,1536]{2,1,0:T(8,128)} %param.18) | copy-start | bytes 2949124
  377.7 50.0 %copy-start.4 = (f32[1,160,1536]{2,1,0:T(8,128)S(1)}, f32[1,160,1536]{2,1,0:T(8,128)}, u32[]{:S(2)}) copy-start(f32[1,160,1536]{2,1,0:T(8,128)} %param.17) | copy-start | bytes 2949124
  427.8 5.8 %copy-start.1 = (bf16[128,2560]{1,0:T(8,128)(2,1)S(1)}, bf16[128,2560]{1,0:T(8,128)(2,1)}, u32[]{:S(2)}) copy-start(bf16[128,2560]{1,0:T(8,128)(2,1)} %param.13) | copy-start | bytes 1966084
Sparse Core Ops, SparseCore 0:
  11.0 108.9 all-gather.4
  143.0 82.4 reduce-scatter.4
  230.1 69.0 all-gather.2
  321.3 104.9 reduce-scatter.2
where the time goes:
time: 441 us; the launch traced here: 440 us
  waiting for transfers between devices  271 us (61%)
  matrix products  54.4 us (12%)
  blocking collectives  29.9 us (7%)
  other arithmetic  24.3 us (6%)
  local copies, waits for them, and re-layouts  24.1 us (5%)
  starting transfers between devices  22.3 us (5%)
  between operations  14 us (3%)
    reduce_scatter x1, waiting for transfers between devices, body(): lax.psum_scatter(second[0], 'dp', scatter_dimension=0, tiled=True)[None]  82.5 us
    all_gather x1, waiting for transfers between devices, body(): lax.all_gather(w_down_shard, 'dp', axis=1, tiled=True)  68.9 us
    all_gather x1, waiting for transfers between devices, body(): lax.all_gather(w_gate_up_shard, 'dp', axis=1, tiled=True)  49 us
    reduce_scatter x1, waiting for transfers between devices, body(): lax.psum_scatter(first[0], 'dp', scatter_dimension=0, tiled=True)[None]  48.6 us
    all_to_all x1, blocking collectives, body(): lax.all_to_all(send_input, 'expert', split_axis=1, concat_axis=1, tiled=T...  29.9 us
    all_to_all x1, waiting for transfers between devices, body(): lax.all_to_all(input_rows.reshape(exp_dev, groups, capacity, width), 'exp...  22.1 us
    dot_general x1, matrix products, body(): jnp.einsum('erd,edf->erf', x_rows, w_gate_up, preferred_element_type=jnp....  12.2 us
    dot_general x1, matrix products, body(): jnp.einsum('erc,erf->ecf', x_rows, pre_grad, preferred_element_type=jnp.f...  11.5 us
  transfers between devices with their start and end apart: 8, of which 5 were waited for; matrix products, arithmetic and copies ran while one was open for 12% of the time, Pallas kernels for 0%

commit v1 on v0

--- a/solution.py
+++ b/solution.py
@@ -77,7 +77,9 @@
     w_down_shard = down_weight.astype(jnp.bfloat16)
     w_gate_up, w_down = (
         lax.all_gather(w_gate_up_shard, "dp", axis=1, tiled=True),
-        lax.all_gather(w_down_shard, "dp", axis=1, tiled=True),
+        jnp.concatenate(
+            lax.all_to_all(jnp.stack([w_down_shard] * lax.axis_size("dp")), "dp", 0, 0), axis=1
+        ),
     )
     recv_input, recv_grad, recv_gate = (
         lax.all_to_all(send_input, "expert", split_axis=1, concat_axis=1, tiled=True),

time: 441 us -> 467 us (1.059)
  blocking collectives: 29.9 us -> 122 us
  waiting for transfers between devices: 271 us -> 204 us
    all_to_all x0 -> x1, blocking collectives: none -> 92 us  [body(): lax.all_to_all(jnp.stack([w_down_shard] * lax.axis_size('dp')), 'dp', 0, 0)]
    all_gather x1 -> x0, waiting for transfers between devices: 68.9 us -> none  [body(): lax.all_gather(w_down_shard, 'dp', axis=1, tiled=True)]
  transfers between devices with their start and end apart: 8 -> 7, of which waited for: 5 -> 4; matrix products, arithmetic and copies ran while one was open for 12% -> 12% of each run, Pallas kernels for 0% -> 0%
where the time goes in v1:
time: 467 us; the launch traced here: 466 us
  waiting for transfers between devices  204 us (44%)
  blocking collectives  122 us (26%)
  matrix products  52.3 us (11%)
  starting transfers between devices  25.2 us (5%)
  local copies, waits for them, and re-layouts  24.1 us (5%)
  other arithmetic  24.1 us (5%)
  between operations  14 us (3%)
    all_to_all x1, blocking collectives, body(): lax.all_to_all(jnp.stack([w_down_shard] * lax.axis_size('dp')), 'dp', 0, 0)  92 us
    reduce_scatter x1, waiting for transfers between devices, body(): lax.psum_scatter(second[0], 'dp', scatter_dimension=0, tiled=True)[None]  82.4 us
    reduce_scatter x1, waiting for transfers between devices, body(): lax.psum_scatter(first[0], 'dp', scatter_dimension=0, tiled=True)[None]  50 us
    all_gather x1, waiting for transfers between devices, body(): lax.all_gather(w_gate_up_shard, 'dp', axis=1, tiled=True)  49.7 us
    all_to_all x1, blocking collectives, body(): lax.all_to_all(send_input, 'expert', split_axis=1, concat_axis=1, tiled=T...  30 us
    all_to_all x1, waiting for transfers between devices, body(): lax.all_to_all(input_rows.reshape(exp_dev, groups, capacity, width), 'exp...  22.1 us
    dot_general x1, matrix products, body(): jnp.einsum('erd,edf->erf', x_rows, w_gate_up, preferred_element_type=jnp....  12.2 us
    dot_general x1, matrix products, body(): jnp.einsum('erf,edf->erd', pre_grad, w_gate_up, preferred_element_type=jn...  11.7 us
  transfers between devices with their start and end apart: 7, of which 4 were waited for; matrix products, arithmetic and copies ran while one was open for 12% of the time, Pallas kernels for 0%

profile of v1, /device:TPU:1, one launch (start us, length us, event | category | flops | bytes accessed | tf_op | source)
XLA Modules:
  0.0 466.0 jit_solution(9435151625381841355)
XLA Ops:
  12.8 2.2 scatter_custom_fusion
  15.7 6.8 %all-to-all-start = ((bf16[1,8,48]{2,0,1:T(2,128)(2,1)}), bf16[1,8,48]{2,0,1:T(2,128)(2,1)S(1)}, u32[]{:S(2)}, u32[]{:S(2)}) async-start(bf16[1,8,48]{2,0,1:T(2,128)(2,1)} %reshape.320), calls=%async_computation | async-start | bytes 8192 | tf_op jit(solution)/shard_map/all_to_all | solution.py:87
  24.0 2.6 gather_fusion.1
  26.6 3.3 gather_fusion
  31.4 3.8 broadcast_select_fusion
  35.2 30.0 %all_to_all.30 = bf16[1,8,48,2560]{3,2,0,1:T(8,128)(2,1)S(1)} all-to-all(bf16[1,8,48,2560]{3,2,0,1:T(8,128)(2,1)} %get-tuple-element.60), channel_id=1, replica_groups=mesh['dp'=16,'expert'=8] {'expert'}, dimensions={1} | all-to-all | bytes 3932160 | tf_op jit(solution)/shard_map/all_to_all | solution.py:85
  65.3 5.0 %all-to-all-start.1 = ((bf16[1,8,48,2560]{3,2,0,1:T(8,128)(2,1)}), bf16[1,8,48,2560]{3,2,0,1:T(8,128)(2,1)}, u32[]{:S(2)}, u32[]{:S(2)}) async-start(bf16[1,8,48,2560]{3,2,0,1:T(8,128)(2,1)} %get-tuple-element.61), calls=%async_computation.1 | async-start | bytes 3932160 | tf_op jit(solution)/shard_map/all_to_all | solution.py:86
  70.4 49.7 %all-gather.2.cloned.1.call-done = bf16[1,2560,3072]{2,1,0:T(8,128)(2,1)} async-done(((bf16[1,160,3072]{2,1,0:T(8,128)(2,1)}), bf16[1,2560,3072]{2,1,0:T(8,128)(2,1)}) %all-gather.2.cloned.1.call-update) | async-done | bytes 15728656 | tf_op jit(solution)/shard_map/all_gather | solution.py:79
  120.1 12.2 %fusion.4 = f32[1,384,3072]{2,1,0:T(8,128)} fusion(bf16[384,2560]{1,0:T(8,128)(2,1)S(1)} %bitcast.82, bf16[1,2560,3072]{2,1,0:T(8,128)(2,1)} %all-gather.2.cloned.1.call-done), kind=kOutput, calls=%fused_computation.13 | convolution fusion | flops 6039797760 | bytes 22413312 | tf_op jit(solution)/shard_map/erd,edf->erf/dot_general | solution.py:92
  132.2 10.6 %convolution_convert_fusion.1 = bf16[1536,2560]{1,0:T(8,128)(2,1)} fusion(bf16[384,2560]{1,0:T(8,128)(2,1)} %bitcast.6, f32[384]{0:T(512)S(1)} %reshape.260, f32[1,384,3072]{2,1,0:T(8,128)} %fusion.4), kind=kOutput, calls=%fused_computation.12 | convolution fusion | flops 3027959808 | bytes 14550528 | tf_op jit(solution)/shard_map/erc,erd->ecd/dot_general | solution.py:111
  142.9 82.4 %reduce-scatter.5.cloned.1.call-done = bf16[96,2560]{1,0:T(8,128)(2,1)} async-done(((bf16[1536,2560]{1,0:T(8,128)(2,1)}), bf16[96,2560]{1,0:T(8,128)(2,1)}) %reduce-scatter.5.cloned.1.call-update) | async-done | bytes 491536 | tf_op jit(solution)/shard_map/reduce_scatter | solution.py:117
  225.3 4.3 multiply_subtract_fusion
  230.4 92.0 %all_to_all.31 = bf16[16,1,96,2560]{3,2,1,0:T(8,128)(2,1)S(1)} all-to-all(bf16[16,1,96,2560]{3,2,1,0:T(8,128)(2,1)S(1)} %stack.2), channel_id=1, replica_groups=mesh['dp'=16,'expert'=8] {'dp'}, dimensions={0} | all-to-all | bytes 15728640 | tf_op jit(solution)/shard_map/all_to_all | solution.py:81
  322.4 6.5 %fusion.19 = (bf16[384,1536]{1,0:T(8,128)(2,1)S(1)}, bf16[384,1536]{1,0:T(8,128)(2,1)S(1)}, bf16[384]{0:T(512)(128)(2,1)S(1)}) fusion(f32[1,384,3072]{2,1,0:T(8,128)} %fusion.4, f32[384]{0:T(512)S(1)} %reshape.260, bf16[384,2560]{1,0:T(8,128)(2,1)} %bitcast.6, bf16[1536,2560]{1,0:T(8,128)(2,1)S(1)} %bitcast.79), kind=kOutput, calls=%fused_computation.36 | convolution fusion | flops 3031105024 | bytes 16910592 | tf_op jit(solution)/shard_map/erd,efd->erf/dot_general | solution.py:100
  330.3 11.4 %convolution_convert_fusion = bf16[2560,3072]{1,0:T(8,128)(2,1)} fusion(bf16[384,2560]{1,0:T(8,128)(2,1)S(1)} %bitcast.83, bf16[384,1536]{1,0:T(8,128)(2,1)S(1)} %get-tuple-element.54, bf16[384,1536]{1,0:T(8,128)(2,1)S(1)} %get-tuple-element.53), kind=kOutput, calls=%fused_computation.7 | convolution fusion | flops 6052380672 | bytes 20054016 | tf_op jit(solution)/shard_map/erc,erf->ecf/dot_general | solution.py:114
  342.5 8.4 %all-to-all-start.5 = ((bf16[1,8,48]{2,0,1:T(2,128)(2,1)}), bf16[1,8,48]{2,0,1:T(2,128)(2,1)S(1)}, u32[]{:S(2)}, u32[]{:S(2)}) async-start(bf16[1,8,48]{2,0,1:T(2,128)(2,1)} %convert_element_type.105), calls=%async_computation.5 | async-start | bytes 8192 | tf_op jit(solution)/shard_map/all_to_all | solution.py:131
  350.9 11.7 %fusion.7 = bf16[384,2560]{1,0:T(8,128)(2,1)} fusion(bf16[1,2560,3072]{2,1,0:T(8,128)(2,1)} %all-gather.2.cloned.1.call-done, bf16[384,1536]{1,0:T(8,128)(2,1)S(1)} %copy-done.10, bf16[384,1536]{1,0:T(8,128)(2,1)S(1)} %copy-done.8), kind=kOutput, calls=%fused_computation.14 | convolution fusion | flops 6045499392 | bytes 20054016 | tf_op jit(solution)/shard_map/erf,edf->erd/dot_general | solution.py:108
  362.5 4.8 %all-to-all-start.4 = ((bf16[1,8,48,2560]{3,2,0,1:T(8,128)(2,1)}), bf16[1,8,48,2560]{3,2,0,1:T(8,128)(2,1)S(1)}, u32[]{:S(2)}, u32[]{:S(2)}) async-start(bf16[1,8,48,2560]{3,2,0,1:T(8,128)(2,1)} %bitcast.84), calls=%async_computation.4 | async-start | bytes 3932160 | tf_op jit(solution)/shard_map/all_to_all | solution.py:124
  370.2 22.1 %all-to-all-done.4 = bf16[1,8,48,2560]{3,2,0,1:T(8,128)(2,1)S(1)} async-done(((bf16[1,8,48,2560]{3,2,0,1:T(8,128)(2,1)}), bf16[1,8,48,2560]{3,2,0,1:T(8,128)(2,1)S(1)}, u32[]{:S(2)}, u32[]{:S(2)}) %all-to-all-start.4) | async-done | bytes 1966112 | tf_op jit(solution)/shard_map/all_to_all | solution.py:124
  392.3 2.5 gather_fusion.2
  394.8 3.1 reshape.256
  397.9 4.4 reduce_sum.34
  402.3 50.0 %reduce-scatter.3.cloned.1.call-done = bf16[160,3072]{1,0:T(8,128)(2,1)} async-done(((bf16[2560,3072]{1,0:T(8,128)(2,1)}), bf16[160,3072]{1,0:T(8,128)(2,1)}) %reduce-scatter.3.cloned.1.call-update) | async-done | bytes 983056 | tf_op jit(solution)/shard_map/reduce_scatter | solution.py:120
  453.7 5.8 %multiply_subtract_fusion.1 = (f32[1,160,1536]{2,1,0:T(8,128)}, f32[1,160,1536]{2,1,0:T(8,128)}, f32[1,160,1536]{2,1,0:T(8,128)}, f32[1,160,1536]{2,1,0:T(8,128)...) fusion(f32[1,160,1536]{2,1,0:T(8,128)S(1)} %copy-done.3, f32[1,160,3072]{2,1,0:T(8,128)S(1)} %bitcast_convert_fusion, ...), kind=kLoop, calls=%fused_computation.46 | loop fusion | flops 7372800 | bytes 13762560 | tf_op jit(solution)/shard_map/sub | solution.py:30
  (69 shorter events, 16.4 us)
Async XLA Ops:
  7.2 16.8 %copy-start = (bf16[128,2560]{1,0:T(8,128)(2,1)S(1)}, bf16[128,2560]{1,0:T(8,128)(2,1)}, u32[]{:S(2)}) copy-start(bf16[128,2560]{1,0:T(8,128)(2,1)} %param.13) | copy-start | bytes 1966084
  7.2 112.9 %all-gather.2.cloned.1.call-start = ((), (), s32[]{:S(2)}) async-start(), calls=%async_computation.8 | async-start | bytes 16711680 | tf_op jit(solution)/shard_map/all_gather | solution.py:79
  8.6 2.4 copy-start.5
  8.6 3.9 copy-start.6
  15.7 19.5 %all-to-all-start = ((bf16[1,8,48]{2,0,1:T(2,128)(2,1)}), bf16[1,8,48]{2,0,1:T(2,128)(2,1)S(1)}, u32[]{:S(2)}, u32[]{:S(2)}) async-start(bf16[1,8,48]{2,0,1:T(2,128)(2,1)} %reshape.320), calls=%async_computation | async-start | bytes 8192 | tf_op jit(solution)/shard_map/all_to_all | solution.py:87
  23.9 2.6 copy-start.2
  65.3 67.0 %all-to-all-start.1 = ((bf16[1,8,48,2560]{3,2,0,1:T(8,128)(2,1)}), bf16[1,8,48,2560]{3,2,0,1:T(8,128)(2,1)}, u32[]{:S(2)}, u32[]{:S(2)}) async-start(bf16[1,8,48,2560]{3,2,0,1:T(8,128)(2,1)} %get-tuple-element.61), calls=%async_computation.1 | async-start | bytes 3932160 | tf_op jit(solution)/shard_map/all_to_all | solution.py:86
  70.3 155.0 %reduce-scatter.5.cloned.1.call-start = ((), (), s32[]{:S(2)}) async-start(), calls=%async_computation.10 | async-start | bytes 8355840 | tf_op jit(solution)/shard_map/reduce_scatter | solution.py:117
  142.8 309.5 %reduce-scatter.3.cloned.1.call-start = ((), (), s32[]{:S(2)}) async-start(), calls=%async_computation.9 | async-start | bytes 16711680 | tf_op jit(solution)/shard_map/reduce_scatter | solution.py:120
  328.9 1.0 copy-start.7
  328.9 1.4 copy-start.9
  341.8 9.1 %copy-start.8 = (bf16[384,1536]{1,0:T(8,128)(2,1)S(1)}, bf16[384,1536]{1,0:T(8,128)(2,1)}, u32[]{:S(2)}) copy-start(bf16[384,1536]{1,0:T(8,128)(2,1)} %copy-done.7) | copy-start | bytes 3538948
  341.8 9.1 %copy-start.10 = (bf16[384,1536]{1,0:T(8,128)(2,1)S(1)}, bf16[384,1536]{1,0:T(8,128)(2,1)}, u32[]{:S(2)}) copy-start(bf16[384,1536]{1,0:T(8,128)(2,1)} %copy-done.9) | copy-start | bytes 3538948
  342.5 20.1 %all-to-all-start.5 = ((bf16[1,8,48]{2,0,1:T(2,128)(2,1)}), bf16[1,8,48]{2,0,1:T(2,128)(2,1)S(1)}, u32[]{:S(2)}, u32[]{:S(2)}) async-start(bf16[1,8,48]{2,0,1:T(2,128)(2,1)} %convert_element_type.105), calls=%async_computation.5 | async-start | bytes 8192 | tf_op jit(solution)/shard_map/all_to_all | solution.py:131
  362.5 29.8 %all-to-all-start.4 = ((bf16[1,8,48,2560]{3,2,0,1:T(8,128)(2,1)}), bf16[1,8,48,2560]{3,2,0,1:T(8,128)(2,1)S(1)}, u32[]{:S(2)}, u32[]{:S(2)}) async-start(bf16[1,8,48,2560]{3,2,0,1:T(8,128)(2,1)} %bitcast.84), calls=%async_computation.4 | async-start | bytes 3932160 | tf_op jit(solution)/shard_map/all_to_all | solution.py:124
  397.9 55.8 %copy-start.3 = (f32[1,160,1536]{2,1,0:T(8,128)S(1)}, f32[1,160,1536]{2,1,0:T(8,128)}, u32[]{:S(2)}) copy-start(f32[1,160,1536]{2,1,0:T(8,128)} %param.18) | copy-start | bytes 2949124
  402.3 51.4 %copy-start.4 = (f32[1,160,1536]{2,1,0:T(8,128)S(1)}, f32[1,160,1536]{2,1,0:T(8,128)}, u32[]{:S(2)}) copy-start(f32[1,160,1536]{2,1,0:T(8,128)} %param.17) | copy-start | bytes 2949124
  453.7 5.8 %copy-start.1 = (bf16[128,2560]{1,0:T(8,128)(2,1)S(1)}, bf16[128,2560]{1,0:T(8,128)(2,1)}, u32[]{:S(2)}) copy-start(bf16[128,2560]{1,0:T(8,128)(2,1)} %param.13) | copy-start | bytes 1966084
Sparse Core Ops, SparseCore 0:
  11.0 108.9 all-gather.1
  142.9 82.3 reduce-scatter.4
  341.9 110.3 reduce-scatter.2
